TPU v7x, 256 devices: a whole 4x4x8 slice. The times are simulated.
256 devices in a mesh: lon: 32 (over x, z_lo, core), lat: 8 (over y, z_hi).
Axes of the slice: x: 4, y: 4, z: 8 (z_hi: 2, z_lo: 4; z = z_hi * 4 + z_lo), core: 2. Of those that a mesh axis runs over, the one named last changes fastest.
Arguments:
- state: float32 [3, 256, 64, 8192], P(None, None, 'lat', 'lon'), may hold values from -6 to 6
- bathymetry: float32 [64, 8192], P('lat', 'lon'), may hold values from 0.5 to 2
- obs_index: int32 [8, 32, 256], P('lat', 'lon'), may hold values from 0 to 2047
- obs_count: int32 [8, 32], P('lat', 'lon'), may hold values from 85 to 256, as said below
- obs_value: float32 [8, 32, 256], P('lat', 'lon'), may hold values from -6 to 6
- obs_sd: float32 [8, 32, 256], P('lat', 'lon'), may hold values from 0.5 to 2
Outputs:
- analysis: float32 [3, 256, 64, 8192], P(None, None, 'lat', 'lon')
Inputs may be any that keep to these rules, and one draw needn't show every extreme that they name: `obs_count`: at least 85 slots of every tile are used; at least one tile uses all 256. `obs_index`: several slots may name the same cell.
All inputs are finite; a program needn't handle non-finite values.
Results may differ from a plain program's by a relative error of at most 0.000051.
Values sent between devices are 32-bit elements; how exact they have to be, the bound alone decides.
No kernel may reach another device: no remote copies, remote signals or barrier semaphores. Data moves between devices by JAX's collectives and lax.ppermute only.
A program may use at most 128 MiB of HBM per device.

v0:
```python
import math
import jax
import jax.numpy as jnp
from jax import lax
from jax.sharding import PartitionSpec as P


def with_halo(value, sides, width, wrap):
    for axis, dim in sides:
        count, length = (lax.axis_size(axis), value.shape[dim])
        up = [(i, (i + 1) % count) for i in range(count if wrap else count - 1)]
        down = [(j, i) for i, j in up]
        last = lax.slice_in_dim(value, length - width, length, axis=dim)
        first = lax.slice_in_dim(value, 0, width, axis=dim)
        before = lax.ppermute(last, axis, up)
        after = lax.ppermute(first, axis, down)
        value = jnp.concatenate([before, value, after], axis=dim)
    return value


def coriolis(rows, total):
    return jnp.sin(math.pi / 3.0 * ((rows.astype(jnp.float32) + 0.5) / total - 0.5))[:, None]


def extend(field, width):
    wide = with_halo(field, (("lat", 2),), width, False)
    return with_halo(wide, (("lon", 3),), width, True)


def new_height(height, flux, keep):
    div = (
        flux[0][:, 1:-1, 2:] - flux[0][:, 1:-1, :-2] + flux[1][:, 2:, 1:-1] - flux[1][:, :-2, 1:-1]
    )
    return (height - 0.25 * div) * keep


def new_wind(east, north, height, fcor, keep):
    grad_x = height[:, 1:-1, 2:] - height[:, 1:-1, :-2]
    grad_y = height[:, 2:, 1:-1] - height[:, :-2, 1:-1]
    east_new = (east + 0.5 * (fcor * north - 0.5 * grad_x)) * keep
    north_new = (north - 0.5 * (fcor * east + 0.5 * grad_y)) * keep
    return (east_new, north_new)


def shards(state, bathymetry, obs_index, obs_count, obs_value, obs_sd):
    members, nrows, ncols = (state.shape[1], state.shape[2], state.shape[3])
    total_rows = nrows * lax.axis_size("lat")
    base = lax.axis_index("lat") * nrows
    fcor = coriolis(base + jnp.arange(nrows), total_rows)
    height, east, north = (state[0], state[1], state[2])
    for step in range(2):
        flux = extend(jnp.stack([bathymetry * east, bathymetry * north]), 1)
        height = new_height(height, flux, 1.0)
        tall = extend(height[None], 1)[0]
        east, north = new_wind(east, north, tall, fcor, 1.0)
    slots = obs_index.shape[2]
    flat_height = height.reshape(members, nrows * ncols)
    hx = jnp.take(flat_height, obs_index.reshape(-1), axis=1)
    valid = (jnp.arange(slots) < obs_count.reshape(())).astype(jnp.float32)
    sigma = obs_sd.reshape(-1) * (
        math.sqrt(slots * lax.axis_size("lat") * lax.axis_size("lon")) / 16.0
    )
    hmean = jnp.mean(hx, axis=0)
    anomal = (hx - hmean) / (math.sqrt(members - 1) * sigma) * valid
    innov = (obs_value.reshape(-1) - hmean) / sigma * valid
    gram = jnp.dot(anomal, anomal.T, precision=lax.Precision.HIGHEST)
    proj = jnp.dot(anomal, innov, precision=lax.Precision.HIGHEST)
    gram, proj = lax.psum((gram, proj), ("lon", "lat"))
    eye = jnp.eye(members, dtype=jnp.float32)
    lower = jnp.linalg.cholesky(gram + eye)
    inv_lower = jax.scipy.linalg.solve_triangular(lower, eye, lower=True)
    weights = jax.scipy.linalg.cho_solve((lower, True), proj)
    transform = inv_lower.T + weights[:, None] / math.sqrt(members - 1)
    fields = jnp.stack([height, east, north])
    center = jnp.mean(fields, axis=1, keepdims=True)
    mixed = jnp.einsum("nm,cnab->cmab", transform, fields - center, precision=lax.Precision.HIGHEST)
    return center + mixed


def solution(mesh):
    return jax.shard_map(
        shards,
        mesh=mesh,
        in_specs=(
            P(None, None, "lat", "lon"),
            P("lat", "lon"),
            P("lat", "lon", None),
            P("lat", "lon"),
            P("lat", "lon", None),
            P("lat", "lon", None),
        ),
        out_specs=P(None, None, "lat", "lon"),
        check_vma=False,
    )
```

profile of v0, /device:TPU:8, one launch (start us, length us, event | category | flops | bytes accessed | tf_op | source)
XLA Modules:
  0.0 587.8 jit_solution(7116847816058828899)
XLA Ops:
  6.5 5.7 fusion.62
  12.2 1.9 copy.68
  14.2 1.3 copy-done.4
  15.9 2.2 copy.43
  18.0 4.2 copy.66
  22.2 4.0 broadcast_multiply_fusion
  27.2 9.1 %collective-permute-start = (f32[2,256,1,256]{1,0,3,2:T(2,128)S(1)}, f32[2,256,1,256]{1,0,3,2:T(2,128)S(1)}, u32[]{:S(2)}, u32[]{:S(2)}) collective-permute-start(f32[2,256,1,256]{1,0,3,2:T(2,128)S(1)} %get-tuple-element.44), channel_id=1, source_target_pairs={{0,1},{1,2},{2,3},{3,4},{4,5},{5,6},{6,7},{8,9},{9,10},{10,11},{11... | collective-permute-start | bytes 1572872 | tf_op jit(solution)/shard_map/ppermute | solution.py:15
  36.3 1.9 collective-permute-start.1
  38.3 12.9 %collective-permute-done = f32[2,256,1,256]{1,0,3,2:T(2,128)S(1)} collective-permute-done((f32[2,256,1,256]{1,0,3,2:T(2,128)S(1)}, f32[2,256,1,256]{1,0,3,2:T(2,128)S(1)}, u32[]{:S(2)}, u32[]{:S(2)}) %collective-permute-start) | collective-permute-done | bytes 524320 | tf_op jit(solution)/shard_map/ppermute | solution.py:15
  51.2 30.3 %collective-permute-done.1 = f32[2,256,1,256]{1,0,3,2:T(2,128)S(1)} collective-permute-done((f32[2,256,1,256]{1,0,3,2:T(2,128)S(1)}, f32[2,256,1,256]{1,0,3,2:T(2,128)S(1)}, u32[]{:S(2)}, u32[]{:S(2)}) %collective-permute-start.1) | collective-permute-done | bytes 524320 | tf_op jit(solution)/shard_map/ppermute | solution.py:16
  81.6 5.9 %collective-permute-start.3 = (f32[2,256,10,1]{1,0,3,2:T(2,128)S(1)}, f32[2,256,10,1]{1,0,3,2:T(2,128)S(1)}, u32[]{:S(2)}, u32[]{:S(2)}) collective-permute-start(f32[2,256,10,1]{1,0,3,2:T(2,128)S(1)} %get-tuple-element.41), channel_id=1, source_target_pairs={{8,0},{16,8},{24,16},{32,24},{40,32},{48,40},{56,48},{64,56},{72,6... | collective-permute-start | bytes 61448 | tf_op jit(solution)/shard_map/ppermute | solution.py:16
  87.5 2.9 copy.67
  90.4 9.7 %pad_maximum_fusion.2 = f32[2,256,10,258]{1,0,3,2:T(2,128)} fusion(f32[2,256,10,1]{1,0,3,2:T(2,128)S(1)} %collective-permute-done.3, f32[2,256,1,256]{1,0,3,2:T(2,128)S(1)} %collective-permute-done.1, f32[1,256,8,256]{1,0,3,2:T(1,128)} %copy-done, f32[1,256,8,256]{1,0,3,2:T(1,128)S(1)} %copy.43, f32[2,256,1,256]{1,0,3,2:T(2,128)S(1)} %collective-permute-done, ...), kind=kLoop, calls=%fused_computation.8 | loop fusion | flops 6604800 | bytes 10567680 | tf_op jit(solution)/shard_map/concatenate | solution.py:17
  100.1 10.4 %fusion.63 = (f32[1,256,10,258]{1,0,3,2:T(1,128)S(1)}, f32[1,256,10,258]{1,0,3,2:T(1,128)}) fusion(f32[2,256,10,258]{1,0,3,2:T(2,128)} %pad_maximum_fusion.2), kind=kLoop, calls=%fused_computation.141 | loop fusion | bytes 10567680 | tf_op jit(solution)/shard_map/slice | solution.py:32
  110.5 2.4 copy_bitcast_fusion
  113.6 9.3 %collective-permute-start.4 = (f32[1,256,1,256]{1,3,2,0:T(8,128)S(1)}, f32[1,256,1,256]{1,3,2,0:T(8,128)S(1)}, u32[]{:S(2)}, u32[]{:S(2)}) collective-permute-start(f32[1,256,1,256]{1,3,2,0:T(8,128)S(1)} %get-tuple-element.52), channel_id=1, source_target_pairs={{0,1},{1,2},{2,3},{3,4},{4,5},{5,6},{6,7},{8,9},{9,10},{10,11},{11... | collective-permute-start | bytes 786440 | tf_op jit(solution)/shard_map/ppermute | solution.py:15
  123.0 1.9 collective-permute-start.5
  125.0 10.7 %collective-permute-done.4 = f32[1,256,1,256]{1,3,2,0:T(8,128)S(1)} collective-permute-done((f32[1,256,1,256]{1,3,2,0:T(8,128)S(1)}, f32[1,256,1,256]{1,3,2,0:T(8,128)S(1)}, u32[]{:S(2)}, u32[]{:S(2)}) %collective-permute-start.4) | collective-permute-done | bytes 262176 | tf_op jit(solution)/shard_map/ppermute | solution.py:15
  135.7 6.7 %collective-permute-done.5 = f32[1,256,1,256]{1,3,2,0:T(8,128)S(1)} collective-permute-done((f32[1,256,1,256]{1,3,2,0:T(8,128)S(1)}, f32[1,256,1,256]{1,3,2,0:T(8,128)S(1)}, u32[]{:S(2)}, u32[]{:S(2)}) %collective-permute-start.5) | collective-permute-done | bytes 262176 | tf_op jit(solution)/shard_map/ppermute | solution.py:16
  142.6 1.5 copy-done.6
  144.1 5.8 collective-permute-start.7
  150.0 3.2 copy.63
  153.8 2.7 copy.47
  156.6 2.4 pad_maximum_fusion.4
  159.3 1.3 copy-done.5
  161.2 2.8 multiply_bitcast_fusion.1
  164.1 6.4 %collective-permute-start.8 = (f32[2,256,1,256]{1,3,2,0:T(8,128)S(1)}, f32[2,256,1,256]{1,3,2,0:T(8,128)S(1)}, u32[]{:S(2)}, u32[]{:S(2)}) collective-permute-start(f32[2,256,1,256]{1,3,2,0:T(8,128)S(1)} %get-tuple-element.42), channel_id=1, source_target_pairs={{0,1},{1,2},{2,3},{3,4},{4,5},{5,6},{6,7},{8,9},{9,10},{10,11},{11... | collective-permute-start | bytes 1572872 | tf_op jit(solution)/shard_map/ppermute | solution.py:15
  170.5 4.3 collective-permute-start.9
  176.5 17.5 %collective-permute-done.8 = f32[2,256,1,256]{1,3,2,0:T(8,128)S(1)} collective-permute-done((f32[2,256,1,256]{1,3,2,0:T(8,128)S(1)}, f32[2,256,1,256]{1,3,2,0:T(8,128)S(1)}, u32[]{:S(2)}, u32[]{:S(2)}) %collective-permute-start.8) | collective-permute-done | bytes 524320 | tf_op jit(solution)/shard_map/ppermute | solution.py:15
  194.2 7.5 %collective-permute-start.11 = (f32[2,256,10,1]{1,0,3,2:T(2,128)S(1)}, f32[2,256,10,1]{1,0,3,2:T(2,128)S(1)}, u32[]{:S(2)}, u32[]{:S(2)}) collective-permute-start(f32[2,256,10,1]{1,0,3,2:T(2,128)S(1)} %copy.50), channel_id=1, source_target_pairs={{8,0},{16,8},{24,16},{32,24},{40,32},{48,40},{56,48},{64,56},{72,6... | collective-permute-start | bytes 61448 | tf_op jit(solution)/shard_map/ppermute | solution.py:16
  202.1 13.5 %collective-permute-done.10 = f32[2,256,10,1]{1,0,3,2:T(2,128)S(1)} collective-permute-done((f32[2,256,10,1]{1,0,3,2:T(2,128)S(1)}, f32[2,256,10,1]{1,0,3,2:T(2,128)S(1)}, u32[]{:S(2)}, u32[]{:S(2)}) %collective-permute-start.10) | collective-permute-done | bytes 20512 | tf_op jit(solution)/shard_map/ppermute | solution.py:15
  215.7 2.1 pad_maximum_fusion.1
  223.9 7.3 %collective-permute-start.12 = (f32[1,256,1,256]{1,3,2,0:T(8,128)}, f32[1,256,1,256]{1,3,2,0:T(8,128)S(1)}, u32[]{:S(2)}, u32[]{:S(2)}) collective-permute-start(f32[1,256,1,256]{1,3,2,0:T(8,128)} %get-tuple-element.50), channel_id=1, source_target_pairs={{0,1},{1,2},{2,3},{3,4},{4,5},{5,6},{6,7},{8,9},{9,10},{10,11},{11... | collective-permute-start | bytes 786440 | tf_op jit(solution)/shard_map/ppermute | solution.py:15
  231.2 5.8 collective-permute-start.13
  237.2 79.0 %psum.15 = f32[256]{0:T(256)S(1)} all-reduce(f32[256]{0:T(256)S(1)} %bitcast.156), channel_id=1, replica_groups=mesh['lon'=32,'lat'=8] {'lon','lat'}, use_global_device_ids=true, to_apply=%region_7.8 | all-reduce | flops 256 | bytes 2048 | tf_op jit(solution)/shard_map/psum | solution.py:68
  316.2 167.4 %all-reduce.3.cloned.1.call-done = f32[256,256]{0,1:T(8,128)} async-done(((f32[256,256]{0,1:T(8,128)}), f32[256,256]{0,1:T(8,128)}) %all-reduce.3.cloned.1.call-update) | async-done | bytes 262160 | tf_op jit(solution)/shard_map/psum | solution.py:68
  485.8 11.7 %cholesky.49 = f32[128,128]{1,0:T(8,128)S(1)} custom-call(f32[128,128]{1,0:T(8,128)S(1)} %cholesky.115), custom_call_target="Cholesky" | custom-call | tf_op jit(solution)/shard_map/jit(cholesky)/cholesky | solution.py:70
  497.5 9.8 %custom-call.21 = f32[1,128,128]{1,2,0:T(8,128)S(1)} custom-call(f32[1,128,128]{2,1,0:T(8,128)S(1)} %get-tuple-element.57), custom_call_target="InvertDiagBlocksLowerTriangular" | custom-call | tf_op jit(solution)/shard_map/jit(cholesky)/cholesky | solution.py:70
  507.8 11.7 %cholesky.103 = f32[128,128]{1,0:T(8,128)S(1)} custom-call(f32[128,128]{1,0:T(8,128)S(1)} %convolution_subtract_fusion.1), custom_call_target="Cholesky" | custom-call | tf_op jit(solution)/shard_map/jit(cholesky)/cholesky | solution.py:70
  522.4 5.1 while.1
  523.0 2.0 bitcast_dynamic-update-slice_fusion.2
  525.6 1.9 bitcast_dynamic-update-slice_fusion.2
  527.5 20.6 %custom-call.22 = f32[2,128,128]{1,2,0:T(8,128)S(1)} custom-call(f32[2,128,128]{2,1,0:T(8,128)} %get-tuple-element.12), custom_call_target="InvertDiagBlocksLowerTriangular" | custom-call | tf_op jit(solution)/shard_map/jit(_solve_triangular)/triangular_solve | solution.py:71
  551.6 5.6 collective-permute-start.15
  557.3 2.7 copy.54
  560.0 2.7 pad_maximum_fusion.5
  567.0 7.1 %add_bitcast_fusion = f32[3,256,8,256]{1,3,2,0:T(8,128)} fusion(f32[3,8,256]{2,1,0:T(8,128)S(1)} %broadcast_multiply_fusion.2, f32[1,256,8,256]{1,3,2,0:T(8,128)S(1)} %get-tuple-element.30, f32[1,256,8,256]{1,3,2,0:T(8,128)S(1)} %get-tuple-element.29, f32[1,256,8,256]{1,3,2,0:T(8,128)S(1)} %bitcast.145, f32[128,256]{1,0:T(8,128)S(1)} %fusion.48, ...), kind=kOutput, calls=%fused_computation.4 | convolution fusion | flops 4838260736 | bytes 12870656 | tf_op jit(solution)/shard_map/nm,cnab->cmab/dot_general | solution.py:76
  574.0 6.6 %copy.59 = f32[3,256,8,256]{3,2,1,0:T(8,128)} copy(f32[3,256,8,256]{1,3,2,0:T(8,128)} %add_bitcast_fusion) | data formatting | bytes 12582912 | tf_op jit(solution)/shard_map/add | solution.py:77
  (124 shorter events, 25.0 us)
Async XLA Ops:
  6.5 477.1 %all-reduce.3.cloned.1.call-start = ((), (), s32[]{:S(2)}) async-start(), calls=%async_computation | async-start | bytes 524288 | tf_op jit(solution)/shard_map/psum | solution.py:68
  12.2 3.3 copy-start.12
  14.2 1.3 copy-start.4
  26.3 55.2 %copy-start = (f32[1,256,8,256]{1,0,3,2:T(1,128)}, f32[1,256,8,256]{1,0,3,2:T(1,128)S(1)}, u32[]{:S(2)}) copy-start(f32[1,256,8,256]{1,0,3,2:T(1,128)S(1)} %broadcast_multiply_fusion) | copy-start | bytes 6291460
  27.2 24.0 %collective-permute-start = (f32[2,256,1,256]{1,0,3,2:T(2,128)S(1)}, f32[2,256,1,256]{1,0,3,2:T(2,128)S(1)}, u32[]{:S(2)}, u32[]{:S(2)}) collective-permute-start(f32[2,256,1,256]{1,0,3,2:T(2,128)S(1)} %get-tuple-element.44), channel_id=1, source_target_pairs={{0,1},{1,2},{2,3},{3,4},{4,5},{5,6},{6,7},{8,9},{9,10},{10,11},{11... | collective-permute-start | bytes 1572872 | tf_op jit(solution)/shard_map/ppermute | solution.py:15
  36.3 45.1 %collective-permute-start.1 = (f32[2,256,1,256]{1,0,3,2:T(2,128)S(1)}, f32[2,256,1,256]{1,0,3,2:T(2,128)S(1)}, u32[]{:S(2)}, u32[]{:S(2)}) collective-permute-start(f32[2,256,1,256]{1,0,3,2:T(2,128)S(1)} %get-tuple-element.45), channel_id=1, source_target_pairs={{1,0},{2,1},{3,2},{4,3},{5,4},{6,5},{7,6},{9,8},{10,9},{11,10},{12... | collective-permute-start | bytes 1572872 | tf_op jit(solution)/shard_map/ppermute | solution.py:16
  81.5 8.9 %collective-permute-start.2 = (f32[2,256,10,1]{1,0,3,2:T(2,128)S(1)}, f32[2,256,10,1]{1,0,3,2:T(2,128)S(1)}, u32[]{:S(2)}, u32[]{:S(2)}) collective-permute-start(f32[2,256,10,1]{1,0,3,2:T(2,128)S(1)} %get-tuple-element.40), channel_id=1, source_target_pairs={{0,8},{8,16},{16,24},{24,32},{32,40},{40,48},{48,56},{56,64},{64,7... | collective-permute-start | bytes 61448 | tf_op jit(solution)/shard_map/ppermute | solution.py:15
  81.6 8.8 %collective-permute-start.3 = (f32[2,256,10,1]{1,0,3,2:T(2,128)S(1)}, f32[2,256,10,1]{1,0,3,2:T(2,128)S(1)}, u32[]{:S(2)}, u32[]{:S(2)}) collective-permute-start(f32[2,256,10,1]{1,0,3,2:T(2,128)S(1)} %get-tuple-element.41), channel_id=1, source_target_pairs={{8,0},{16,8},{24,16},{32,24},{40,32},{48,40},{56,48},{64,56},{72,6... | collective-permute-start | bytes 61448 | tf_op jit(solution)/shard_map/ppermute | solution.py:16
  110.5 2.4 copy-start.8
  112.9 12.0 %copy-start.16 = (s32[1,1,256]{2,1,0:T(1,128)S(1)}, s32[1,1,256]{2,1,0:T(1,128)}, u32[]{:S(2)}) copy-start(s32[1,1,256]{2,1,0:T(1,128)} %param.8) | copy-start | bytes 3076
  113.6 29.0 %copy-start.2 = (f32[256,8,256]{0,2,1:T(8,128)}, f32[256,8,256]{0,2,1:T(8,128)S(1)}, u32[]{:S(2)}) copy-start(f32[256,8,256]{0,2,1:T(8,128)S(1)} %fusion.27) | copy-start | bytes 6291460
  113.6 22.0 %collective-permute-start.4 = (f32[1,256,1,256]{1,3,2,0:T(8,128)S(1)}, f32[1,256,1,256]{1,3,2,0:T(8,128)S(1)}, u32[]{:S(2)}, u32[]{:S(2)}) collective-permute-start(f32[1,256,1,256]{1,3,2,0:T(8,128)S(1)} %get-tuple-element.52), channel_id=1, source_target_pairs={{0,1},{1,2},{2,3},{3,4},{4,5},{5,6},{6,7},{8,9},{9,10},{10,11},{11... | collective-permute-start | bytes 786440 | tf_op jit(solution)/shard_map/ppermute | solution.py:15
  123.0 19.3 %collective-permute-start.5 = (f32[1,256,1,256]{1,3,2,0:T(8,128)S(1)}, f32[1,256,1,256]{1,3,2,0:T(8,128)S(1)}, u32[]{:S(2)}, u32[]{:S(2)}) collective-permute-start(f32[1,256,1,256]{1,3,2,0:T(8,128)S(1)} %get-tuple-element.53), channel_id=1, source_target_pairs={{1,0},{2,1},{3,2},{4,3},{5,4},{6,5},{7,6},{9,8},{10,9},{11,10},{12... | collective-permute-start | bytes 786440 | tf_op jit(solution)/shard_map/ppermute | solution.py:16
  142.6 1.5 copy-start.6
  144.1 12.4 %collective-permute-start.6 = (f32[1,256,10,1]{1,3,2,0:T(1,128)S(1)}, f32[1,256,10,1]{1,3,2,0:T(1,128)S(1)}, u32[]{:S(2)}, u32[]{:S(2)}) collective-permute-start(f32[1,256,10,1]{1,3,2,0:T(1,128)S(1)} %get-tuple-element.48), channel_id=1, source_target_pairs={{0,8},{8,16},{16,24},{24,32},{32,40},{40,48},{48,56},{56,64},{64,7... | collective-permute-start | bytes 30728 | tf_op jit(solution)/shard_map/ppermute | solution.py:15
  144.1 12.5 %collective-permute-start.7 = (f32[1,256,10,1]{1,3,2,0:T(1,128)S(1)}, f32[1,256,10,1]{1,3,2,0:T(1,128)S(1)}, u32[]{:S(2)}, u32[]{:S(2)}) collective-permute-start(f32[1,256,10,1]{1,3,2,0:T(1,128)S(1)} %get-tuple-element.49), channel_id=1, source_target_pairs={{8,0},{16,8},{24,16},{32,24},{40,32},{48,40},{56,48},{64,56},{72,6... | collective-permute-start | bytes 30728 | tf_op jit(solution)/shard_map/ppermute | solution.py:16
  150.0 9.3 %copy-start.18 = (f32[8]{0:T(128)}, f32[8]{0:T(128)S(1)}, u32[]{:S(2)}) copy-start(f32[8]{0:T(128)S(1)} %multiply_sine_fusion) | copy-start | bytes 100
  150.0 3.8 copy-start.7
  159.0 1.6 copy-start.5
  159.0 2.2 copy-start.11
  164.0 30.0 %copy-start.1 = (f32[1,256,8,256]{1,3,2,0:T(8,128)}, f32[1,256,8,256]{1,3,2,0:T(8,128)S(1)}, u32[]{:S(2)}) copy-start(f32[1,256,8,256]{1,3,2,0:T(8,128)S(1)} %get-tuple-element.27) | copy-start | bytes 6291460
  164.0 11.9 %copy-start.20 = (f32[1,1,256]{2,1,0:T(1,128)S(1)}, f32[1,1,256]{2,1,0:T(1,128)}, u32[]{:S(2)}) copy-start(f32[1,1,256]{2,1,0:T(1,128)} %param.11) | copy-start | bytes 3076
  164.1 29.9 %collective-permute-start.8 = (f32[2,256,1,256]{1,3,2,0:T(8,128)S(1)}, f32[2,256,1,256]{1,3,2,0:T(8,128)S(1)}, u32[]{:S(2)}, u32[]{:S(2)}) collective-permute-start(f32[2,256,1,256]{1,3,2,0:T(8,128)S(1)} %get-tuple-element.42), channel_id=1, source_target_pairs={{0,1},{1,2},{2,3},{3,4},{4,5},{5,6},{6,7},{8,9},{9,10},{10,11},{11... | collective-permute-start | bytes 1572872 | tf_op jit(solution)/shard_map/ppermute | solution.py:15
  170.5 23.5 %collective-permute-start.9 = (f32[2,256,1,256]{1,3,2,0:T(8,128)S(1)}, f32[2,256,1,256]{1,3,2,0:T(8,128)S(1)}, u32[]{:S(2)}, u32[]{:S(2)}) collective-permute-start(f32[2,256,1,256]{1,3,2,0:T(8,128)S(1)} %get-tuple-element.43), channel_id=1, source_target_pairs={{1,0},{2,1},{3,2},{4,3},{5,4},{6,5},{7,6},{9,8},{10,9},{11,10},{12... | collective-permute-start | bytes 1572872 | tf_op jit(solution)/shard_map/ppermute | solution.py:16
  194.0 21.6 %collective-permute-start.10 = (f32[2,256,10,1]{1,0,3,2:T(2,128)S(1)}, f32[2,256,10,1]{1,0,3,2:T(2,128)S(1)}, u32[]{:S(2)}, u32[]{:S(2)}) collective-permute-start(f32[2,256,10,1]{1,0,3,2:T(2,128)S(1)} %copy.49), channel_id=1, source_target_pairs={{0,8},{8,16},{16,24},{24,32},{32,40},{40,48},{48,56},{56,64},{64,7... | collective-permute-start | bytes 61448 | tf_op jit(solution)/shard_map/ppermute | solution.py:15
  194.2 21.5 %collective-permute-start.11 = (f32[2,256,10,1]{1,0,3,2:T(2,128)S(1)}, f32[2,256,10,1]{1,0,3,2:T(2,128)S(1)}, u32[]{:S(2)}, u32[]{:S(2)}) collective-permute-start(f32[2,256,10,1]{1,0,3,2:T(2,128)S(1)} %copy.50), channel_id=1, source_target_pairs={{8,0},{16,8},{24,16},{32,24},{40,32},{48,40},{56,48},{64,56},{72,6... | collective-permute-start | bytes 61448 | tf_op jit(solution)/shard_map/ppermute | solution.py:16
  217.9 1.6 copy-start.3
  220.1 1.2 copy-start.13
  220.1 1.3 copy-start.17
  220.1 1.3 copy-start.21
  220.1 1.4 copy-start.14
  220.2 1.4 copy-start.15
  223.9 298.5 %copy-start.22 = (s32[2]{0:T(128)S(1)}, s32[2]{0:T(128)}, u32[]{:S(2)}) copy-start(s32[2]{0:T(128)} %iota_multiply_fusion) | copy-start | bytes 28
  223.9 326.5 %collective-permute-start.12 = (f32[1,256,1,256]{1,3,2,0:T(8,128)}, f32[1,256,1,256]{1,3,2,0:T(8,128)S(1)}, u32[]{:S(2)}, u32[]{:S(2)}) collective-permute-start(f32[1,256,1,256]{1,3,2,0:T(8,128)} %get-tuple-element.50), channel_id=1, source_target_pairs={{0,1},{1,2},{2,3},{3,4},{4,5},{5,6},{6,7},{8,9},{9,10},{10,11},{11... | collective-permute-start | bytes 786440 | tf_op jit(solution)/shard_map/ppermute | solution.py:15
  231.2 319.2 %collective-permute-start.13 = (f32[1,256,1,256]{1,3,2,0:T(8,128)}, f32[1,256,1,256]{1,3,2,0:T(8,128)}, u32[]{:S(2)}, u32[]{:S(2)}) collective-permute-start(f32[1,256,1,256]{1,3,2,0:T(8,128)} %get-tuple-element.51), channel_id=1, source_target_pairs={{1,0},{2,1},{3,2},{4,3},{5,4},{6,5},{7,6},{9,8},{10,9},{11,10},{12... | collective-permute-start | bytes 786440 | tf_op jit(solution)/shard_map/ppermute | solution.py:16
  551.6 8.5 %collective-permute-start.14 = (f32[1,256,10,1]{1,3,2,0:T(1,128)S(1)}, f32[1,256,10,1]{1,3,2,0:T(1,128)S(1)}, u32[]{:S(2)}, u32[]{:S(2)}) collective-permute-start(f32[1,256,10,1]{1,3,2,0:T(1,128)S(1)} %get-tuple-element.46), channel_id=1, source_target_pairs={{0,8},{8,16},{16,24},{24,32},{32,40},{40,48},{48,56},{56,64},{64,7... | collective-permute-start | bytes 30728 | tf_op jit(solution)/shard_map/ppermute | solution.py:15
  551.6 8.4 %collective-permute-start.15 = (f32[1,256,10,1]{1,3,2,0:T(1,128)S(1)}, f32[1,256,10,1]{1,3,2,0:T(1,128)S(1)}, u32[]{:S(2)}, u32[]{:S(2)}) collective-permute-start(f32[1,256,10,1]{1,3,2,0:T(1,128)S(1)} %get-tuple-element.47), channel_id=1, source_target_pairs={{8,0},{16,8},{24,16},{32,24},{40,32},{48,40},{56,48},{64,56},{72,6... | collective-permute-start | bytes 30728 | tf_op jit(solution)/shard_map/ppermute | solution.py:16
  562.7 1.6 copy-start.9
  562.7 2.2 copy-start.10
  562.7 2.2 copy-start.19
Sparse Core Ops, SparseCore 0:
  223.2 260.4 all-reduce.2
where the time goes:
time: 594 us; the launch traced here: 588 us
  waiting for transfers between devices  259 us (44%)
  other arithmetic  90 us (15%)
  blocking collectives  79 us (13%)
  starting transfers between devices  71.1 us (12%)
  local copies, waits for them, and re-layouts  61.1 us (10%)
  between operations  16.3 us (3%)
  matrix products  11.2 us (2%)
    psum x1, waiting for transfers between devices, shards(): gram, proj = lax.psum((gram, proj), ('lon', 'lat'))  167 us
    psum x1, blocking collectives, shards(): gram, proj = lax.psum((gram, proj), ('lon', 'lat'))  79 us
    ppermute x8, waiting for transfers between devices, with_halo(): before = lax.ppermute(last, axis, up)  54.6 us
    ppermute x8, starting transfers between devices, with_halo(): after = lax.ppermute(first, axis, down)  38.8 us
    ppermute x8, waiting for transfers between devices, with_halo(): after = lax.ppermute(first, axis, down)  37 us
    another operation x7, other arithmetic, shards(): lower = jnp.linalg.cholesky(gram + eye)  34.7 us
    ppermute x8, starting transfers between devices, with_halo(): before = lax.ppermute(last, axis, up)  32.3 us
    another operation x3, other arithmetic, shards(): inv_lower = jax.scipy.linalg.solve_triangular(lower, eye, lower=True)  21.2 us
  transfers between devices with their start and end apart: 17, of which 7 were waited for; matrix products, arithmetic and copies ran while one was open for 14% of the time, Pallas kernels for 0%

commit v1 on v0

--- a/solution.py
+++ b/solution.py
@@ -65,7 +65,7 @@
     innov = (obs_value.reshape(-1) - hmean) / sigma * valid
     gram = jnp.dot(anomal, anomal.T, precision=lax.Precision.HIGHEST)
     proj = jnp.dot(anomal, innov, precision=lax.Precision.HIGHEST)
-    gram, proj = lax.psum((gram, proj), ("lon", "lat"))
+    gram, proj = lax.psum(lax.psum((gram, proj), "lon"), "lat")
     eye = jnp.eye(members, dtype=jnp.float32)
     lower = jnp.linalg.cholesky(gram + eye)
     inv_lower = jax.scipy.linalg.solve_triangular(lower, eye, lower=True)

time: 594 us -> 719 us (1.21)
  waiting for transfers between devices: 259 us -> 358 us
  blocking collectives: 79 us -> 94.4 us
    psum x1 -> x2, waiting for transfers between devices: 167 us -> 253 us  [shards(): gram, proj = lax.psum(lax.psum((gram, proj), 'lon'), 'lat')]
    psum x1 -> x2, blocking collectives: 79 us -> 94.4 us  [shards(): gram, proj = lax.psum(lax.psum((gram, proj), 'lon'), 'lat')]
    ppermute x8, waiting for transfers between devices: 54.6 us -> 62.9 us  [with_halo(): before = lax.ppermute(last, axis, up)]
    unnamed x52 -> x58, local copies, waits for them, and re-layouts: 20.5 us -> 23.2 us
  transfers between devices with their start and end apart: 17 -> 18, of which waited for: 7 -> 10; matrix products, arithmetic and copies ran while one was open for 14% -> 4% of each run, Pallas kernels for 0% -> 0%
where the time goes in v1:
time: 719 us; the launch traced here: 711 us
  waiting for transfers between devices  358 us (50%)
  blocking collectives  94.4 us (13%)
  other arithmetic  91.4 us (13%)
  starting transfers between devices  71.3 us (10%)
  local copies, waits for them, and re-layouts  66.9 us (9%)
  between operations  16.4 us (2%)
  matrix products  12.6 us (2%)
    psum x2, waiting for transfers between devices, shards(): gram, proj = lax.psum(lax.psum((gram, proj), 'lon'), 'lat')  253 us
    psum x2, blocking collectives, shards(): gram, proj = lax.psum(lax.psum((gram, proj), 'lon'), 'lat')  94.4 us
    ppermute x8, waiting for transfers between devices, with_halo(): before = lax.ppermute(last, axis, up)  62.9 us
    ppermute x8, waiting for transfers between devices, with_halo(): after = lax.ppermute(first, axis, down)  41.4 us
    ppermute x8, starting transfers between devices, with_halo(): after = lax.ppermute(first, axis, down)  39.1 us
    another operation x7, other arithmetic, shards(): lower = jnp.linalg.cholesky(gram + eye)  34.8 us
    ppermute x8, starting transfers between devices, with_halo(): before = lax.ppermute(last, axis, up)  32.1 us
    unnamed x58, local copies, waits for them, and re-layouts  23.2 us
  transfers between devices with their start and end apart: 18, of which 10 were waited for; matrix products, arithmetic and copies ran while one was open for 4% of the time, Pallas kernels for 0%

profile of v1, /device:TPU:8, one launch (start us, length us, event | category | flops | bytes accessed | tf_op | source)
XLA Modules:
  0.0 710.7 jit_solution(11304151418569631551)
XLA Ops:
  6.5 5.7 fusion.62
  12.3 1.9 copy.68
  15.9 2.2 copy.43
  18.1 4.3 copy.66
  22.4 4.0 broadcast_multiply_fusion
  27.3 9.1 %collective-permute-start = (f32[2,256,1,256]{1,0,3,2:T(2,128)S(1)}, f32[2,256,1,256]{1,0,3,2:T(2,128)S(1)}, u32[]{:S(2)}, u32[]{:S(2)}) collective-permute-start(f32[2,256,1,256]{1,0,3,2:T(2,128)S(1)} %get-tuple-element.44), channel_id=1, source_target_pairs={{0,1},{1,2},{2,3},{3,4},{4,5},{5,6},{6,7},{8,9},{9,10},{10,11},{11... | collective-permute-start | bytes 1572872 | tf_op jit(solution)/shard_map/ppermute | solution.py:15
  36.5 1.9 collective-permute-start.1
  38.4 12.9 %collective-permute-done = f32[2,256,1,256]{1,0,3,2:T(2,128)S(1)} collective-permute-done((f32[2,256,1,256]{1,0,3,2:T(2,128)S(1)}, f32[2,256,1,256]{1,0,3,2:T(2,128)S(1)}, u32[]{:S(2)}, u32[]{:S(2)}) %collective-permute-start) | collective-permute-done | bytes 524320 | tf_op jit(solution)/shard_map/ppermute | solution.py:15
  51.3 30.3 %collective-permute-done.1 = f32[2,256,1,256]{1,0,3,2:T(2,128)S(1)} collective-permute-done((f32[2,256,1,256]{1,0,3,2:T(2,128)S(1)}, f32[2,256,1,256]{1,0,3,2:T(2,128)S(1)}, u32[]{:S(2)}, u32[]{:S(2)}) %collective-permute-start.1) | collective-permute-done | bytes 524320 | tf_op jit(solution)/shard_map/ppermute | solution.py:16
  81.7 6.2 collective-permute-start.3
  88.0 2.9 copy.67
  90.9 9.7 %pad_maximum_fusion.2 = f32[2,256,10,258]{1,0,3,2:T(2,128)} fusion(f32[2,256,10,1]{1,0,3,2:T(2,128)S(1)} %collective-permute-done.3, f32[2,256,1,256]{1,0,3,2:T(2,128)S(1)} %collective-permute-done.1, f32[1,256,8,256]{1,0,3,2:T(1,128)} %copy-done, f32[1,256,8,256]{1,0,3,2:T(1,128)S(1)} %copy.43, f32[2,256,1,256]{1,0,3,2:T(2,128)S(1)} %collective-permute-done, ...), kind=kLoop, calls=%fused_computation.8 | loop fusion | flops 6604800 | bytes 10567680 | tf_op jit(solution)/shard_map/concatenate | solution.py:17
  100.7 10.3 %fusion.63 = (f32[1,256,10,258]{1,0,3,2:T(1,128)S(1)}, f32[1,256,10,258]{1,0,3,2:T(1,128)}) fusion(f32[2,256,10,258]{1,0,3,2:T(2,128)} %pad_maximum_fusion.2), kind=kLoop, calls=%fused_computation.141 | loop fusion | bytes 10567680 | tf_op jit(solution)/shard_map/slice | solution.py:32
  111.0 2.4 copy_bitcast_fusion
  114.1 9.3 %collective-permute-start.4 = (f32[1,256,1,256]{1,3,2,0:T(8,128)S(1)}, f32[1,256,1,256]{1,3,2,0:T(8,128)S(1)}, u32[]{:S(2)}, u32[]{:S(2)}) collective-permute-start(f32[1,256,1,256]{1,3,2,0:T(8,128)S(1)} %get-tuple-element.52), channel_id=1, source_target_pairs={{0,1},{1,2},{2,3},{3,4},{4,5},{5,6},{6,7},{8,9},{9,10},{10,11},{11... | collective-permute-start | bytes 786440 | tf_op jit(solution)/shard_map/ppermute | solution.py:15
  123.4 1.9 collective-permute-start.5
  125.4 10.7 %collective-permute-done.4 = f32[1,256,1,256]{1,3,2,0:T(8,128)S(1)} collective-permute-done((f32[1,256,1,256]{1,3,2,0:T(8,128)S(1)}, f32[1,256,1,256]{1,3,2,0:T(8,128)S(1)}, u32[]{:S(2)}, u32[]{:S(2)}) %collective-permute-start.4) | collective-permute-done | bytes 262176 | tf_op jit(solution)/shard_map/ppermute | solution.py:15
  136.1 6.7 collective-permute-done.5
  144.6 5.8 collective-permute-start.7
  150.5 3.1 copy.63
  154.2 2.7 copy.47
  157.0 2.4 pad_maximum_fusion.4
  161.6 2.8 multiply_bitcast_fusion.1
  164.5 6.3 collective-permute-start.8
  170.8 4.3 collective-permute-start.9
  177.0 17.3 %collective-permute-done.8 = f32[2,256,1,256]{1,3,2,0:T(8,128)S(1)} collective-permute-done((f32[2,256,1,256]{1,3,2,0:T(8,128)S(1)}, f32[2,256,1,256]{1,3,2,0:T(8,128)S(1)}, u32[]{:S(2)}, u32[]{:S(2)}) %collective-permute-start.8) | collective-permute-done | bytes 524320 | tf_op jit(solution)/shard_map/ppermute | solution.py:15
  194.5 7.5 %collective-permute-start.11 = (f32[2,256,10,1]{1,0,3,2:T(2,128)S(1)}, f32[2,256,10,1]{1,0,3,2:T(2,128)S(1)}, u32[]{:S(2)}, u32[]{:S(2)}) collective-permute-start(f32[2,256,10,1]{1,0,3,2:T(2,128)S(1)} %copy.50), channel_id=1, source_target_pairs={{8,0},{16,8},{24,16},{32,24},{40,32},{48,40},{56,48},{64,56},{72,6... | collective-permute-start | bytes 61448 | tf_op jit(solution)/shard_map/ppermute | solution.py:16
  202.5 13.5 %collective-permute-done.10 = f32[2,256,10,1]{1,0,3,2:T(2,128)S(1)} collective-permute-done((f32[2,256,10,1]{1,0,3,2:T(2,128)S(1)}, f32[2,256,10,1]{1,0,3,2:T(2,128)S(1)}, u32[]{:S(2)}, u32[]{:S(2)}) %collective-permute-start.10) | collective-permute-done | bytes 20512 | tf_op jit(solution)/shard_map/ppermute | solution.py:15
  216.1 2.1 pad_maximum_fusion.1
  221.3 7.2 %collective-permute-start.12 = (f32[1,256,1,256]{1,3,2,0:T(8,128)}, f32[1,256,1,256]{1,3,2,0:T(8,128)S(1)}, u32[]{:S(2)}, u32[]{:S(2)}) collective-permute-start(f32[1,256,1,256]{1,3,2,0:T(8,128)} %get-tuple-element.50), channel_id=1, source_target_pairs={{0,1},{1,2},{2,3},{3,4},{4,5},{5,6},{6,7},{8,9},{9,10},{10,11},{11... | collective-permute-start | bytes 786440 | tf_op jit(solution)/shard_map/ppermute | solution.py:15
  228.5 5.8 collective-permute-start.13
  237.2 8.4 %collective-permute-done.12 = f32[1,256,1,256]{1,3,2,0:T(8,128)S(1)} collective-permute-done((f32[1,256,1,256]{1,3,2,0:T(8,128)}, f32[1,256,1,256]{1,3,2,0:T(8,128)S(1)}, u32[]{:S(2)}, u32[]{:S(2)}) %collective-permute-start.12) | collective-permute-done | bytes 262176 | tf_op jit(solution)/shard_map/ppermute | solution.py:15
  245.6 4.4 collective-permute-done.13
  252.0 5.6 collective-permute-start.15
  257.8 67.4 %psum.30 = f32[256]{0:T(256)S(1)} all-reduce(f32[256]{0:T(256)S(1)} %bitcast.156), channel_id=1, replica_groups=mesh['lon'=32,'lat'=8] {'lon'}, use_global_device_ids=true, to_apply=%region_8.9 | all-reduce | flops 256 | bytes 2048 | tf_op jit(solution)/shard_map/psum | solution.py:68
  325.2 27.1 %psum.31 = f32[256]{0:T(256)S(1)} all-reduce(f32[256]{0:T(256)S(1)} %psum.30), channel_id=1, replica_groups=mesh['lon'=32,'lat'=8] {'lat'}, use_global_device_ids=true, to_apply=%region_9.10 | all-reduce | flops 256 | bytes 2048 | tf_op jit(solution)/shard_map/psum | solution.py:68
  352.3 5.9 copy.54
  358.2 155.7 %all-reduce.4.cloned.1.call-done = f32[256,256]{0,1:T(8,128)} async-done(((f32[256,256]{0,1:T(8,128)}), f32[256,256]{0,1:T(8,128)}) %all-reduce.4.cloned.1.call-update) | async-done | bytes 262160 | tf_op jit(solution)/shard_map/psum | solution.py:68
  514.0 4.8 pad_maximum_fusion.5
  524.2 97.6 %all-reduce.6.cloned.1.call-done = f32[256,256]{0,1:T(8,128)} async-done(((f32[256,256]{0,1:T(8,128)}), f32[256,256]{0,1:T(8,128)}) %all-reduce.6.cloned.1.call-update) | async-done | bytes 262160 | tf_op jit(solution)/shard_map/psum | solution.py:68
  623.9 11.7 %cholesky.49 = f32[128,128]{1,0:T(8,128)S(1)} custom-call(f32[128,128]{1,0:T(8,128)S(1)} %cholesky.115), custom_call_target="Cholesky" | custom-call | tf_op jit(solution)/shard_map/jit(cholesky)/cholesky | solution.py:70
  635.6 9.8 %custom-call.21 = f32[1,128,128]{1,2,0:T(8,128)S(1)} custom-call(f32[1,128,128]{2,1,0:T(8,128)S(1)} %get-tuple-element.57), custom_call_target="InvertDiagBlocksLowerTriangular" | custom-call | tf_op jit(solution)/shard_map/jit(cholesky)/cholesky | solution.py:70
  645.9 11.9 %cholesky.103 = f32[128,128]{1,0:T(8,128)S(1)} custom-call(f32[128,128]{1,0:T(8,128)S(1)} %convolution_subtract_fusion.1), custom_call_target="Cholesky" | custom-call | tf_op jit(solution)/shard_map/jit(cholesky)/cholesky | solution.py:70
  660.5 5.1 while.1
  661.2 1.9 bitcast_dynamic-update-slice_fusion.2
  665.6 20.5 %custom-call.22 = f32[2,128,128]{1,2,0:T(8,128)S(1)} custom-call(f32[2,128,128]{2,1,0:T(8,128)} %get-tuple-element.12), custom_call_target="InvertDiagBlocksLowerTriangular" | custom-call | tf_op jit(solution)/shard_map/jit(_solve_triangular)/triangular_solve | solution.py:71
  688.3 8.5 %add_bitcast_fusion = f32[3,256,8,256]{1,3,2,0:T(8,128)} fusion(f32[3,8,256]{2,1,0:T(8,128)S(1)} %broadcast_multiply_fusion.2, f32[1,256,8,256]{1,3,2,0:T(8,128)} %copy-done.5, f32[1,256,8,256]{1,3,2,0:T(8,128)} %copy-done.4, f32[1,256,8,256]{1,3,2,0:T(8,128)S(1)} %bitcast.145, f32[128,256]{1,0:T(8,128)S(1)} %fusion.48, f32[128,256]{1,0:T(8,128)S(1)} %fusion.40, ...), kind=kOutput, calls=%fused_computation.4 | convolution fusion | flops 4838260736 | bytes 12870656 | tf_op jit(solution)/shard_map/nm,cnab->cmab/dot_general | solution.py:76
  696.8 6.6 copy.59
  (134 shorter events, 32.8 us)
Async XLA Ops:
  6.5 507.4 %all-reduce.4.cloned.1.call-start = ((), (), s32[]{:S(2)}) async-start(), calls=%async_computation | async-start | bytes 524288 | tf_op jit(solution)/shard_map/psum | solution.py:68
  12.3 3.3 copy-start.15
  14.2 1.3 copy-start.6
  26.4 55.2 %copy-start = (f32[1,256,8,256]{1,0,3,2:T(1,128)}, f32[1,256,8,256]{1,0,3,2:T(1,128)S(1)}, u32[]{:S(2)}) copy-start(f32[1,256,8,256]{1,0,3,2:T(1,128)S(1)} %broadcast_multiply_fusion) | copy-start | bytes 6291460
  27.3 24.0 %collective-permute-start = (f32[2,256,1,256]{1,0,3,2:T(2,128)S(1)}, f32[2,256,1,256]{1,0,3,2:T(2,128)S(1)}, u32[]{:S(2)}, u32[]{:S(2)}) collective-permute-start(f32[2,256,1,256]{1,0,3,2:T(2,128)S(1)} %get-tuple-element.44), channel_id=1, source_target_pairs={{0,1},{1,2},{2,3},{3,4},{4,5},{5,6},{6,7},{8,9},{9,10},{10,11},{11... | collective-permute-start | bytes 1572872 | tf_op jit(solution)/shard_map/ppermute | solution.py:15
  36.5 45.1 %collective-permute-start.1 = (f32[2,256,1,256]{1,0,3,2:T(2,128)S(1)}, f32[2,256,1,256]{1,0,3,2:T(2,128)S(1)}, u32[]{:S(2)}, u32[]{:S(2)}) collective-permute-start(f32[2,256,1,256]{1,0,3,2:T(2,128)S(1)} %get-tuple-element.45), channel_id=1, source_target_pairs={{1,0},{2,1},{3,2},{4,3},{5,4},{6,5},{7,6},{9,8},{10,9},{11,10},{12... | collective-permute-start | bytes 1572872 | tf_op jit(solution)/shard_map/ppermute | solution.py:16
  81.6 9.3 %collective-permute-start.2 = (f32[2,256,10,1]{1,0,3,2:T(2,128)S(1)}, f32[2,256,10,1]{1,0,3,2:T(2,128)S(1)}, u32[]{:S(2)}, u32[]{:S(2)}) collective-permute-start(f32[2,256,10,1]{1,0,3,2:T(2,128)S(1)} %get-tuple-element.40), channel_id=1, source_target_pairs={{0,8},{8,16},{16,24},{24,32},{32,40},{40,48},{48,56},{56,64},{64,7... | collective-permute-start | bytes 61448 | tf_op jit(solution)/shard_map/ppermute | solution.py:15
  81.7 9.2 %collective-permute-start.3 = (f32[2,256,10,1]{1,0,3,2:T(2,128)S(1)}, f32[2,256,10,1]{1,0,3,2:T(2,128)S(1)}, u32[]{:S(2)}, u32[]{:S(2)}) collective-permute-start(f32[2,256,10,1]{1,0,3,2:T(2,128)S(1)} %get-tuple-element.41), channel_id=1, source_target_pairs={{8,0},{16,8},{24,16},{32,24},{40,32},{48,40},{56,48},{64,56},{72,6... | collective-permute-start | bytes 61448 | tf_op jit(solution)/shard_map/ppermute | solution.py:16
  111.0 2.4 copy-start.11
  113.4 12.0 %copy-start.19 = (s32[1,1,256]{2,1,0:T(1,128)S(1)}, s32[1,1,256]{2,1,0:T(1,128)}, u32[]{:S(2)}) copy-start(s32[1,1,256]{2,1,0:T(1,128)} %param.8) | copy-start | bytes 3076
  114.1 29.0 %copy-start.2 = (f32[256,8,256]{0,2,1:T(8,128)}, f32[256,8,256]{0,2,1:T(8,128)S(1)}, u32[]{:S(2)}) copy-start(f32[256,8,256]{0,2,1:T(8,128)S(1)} %fusion.27) | copy-start | bytes 6291460
  114.1 22.0 %collective-permute-start.4 = (f32[1,256,1,256]{1,3,2,0:T(8,128)S(1)}, f32[1,256,1,256]{1,3,2,0:T(8,128)S(1)}, u32[]{:S(2)}, u32[]{:S(2)}) collective-permute-start(f32[1,256,1,256]{1,3,2,0:T(8,128)S(1)} %get-tuple-element.52), channel_id=1, source_target_pairs={{0,1},{1,2},{2,3},{3,4},{4,5},{5,6},{6,7},{8,9},{9,10},{10,11},{11... | collective-permute-start | bytes 786440 | tf_op jit(solution)/shard_map/ppermute | solution.py:15
  123.4 19.4 %collective-permute-start.5 = (f32[1,256,1,256]{1,3,2,0:T(8,128)S(1)}, f32[1,256,1,256]{1,3,2,0:T(8,128)S(1)}, u32[]{:S(2)}, u32[]{:S(2)}) collective-permute-start(f32[1,256,1,256]{1,3,2,0:T(8,128)S(1)} %get-tuple-element.53), channel_id=1, source_target_pairs={{1,0},{2,1},{3,2},{4,3},{5,4},{6,5},{7,6},{9,8},{10,9},{11,10},{12... | collective-permute-start | bytes 786440 | tf_op jit(solution)/shard_map/ppermute | solution.py:16
  143.1 1.5 copy-start.9
  144.6 12.4 %collective-permute-start.6 = (f32[1,256,10,1]{1,3,2,0:T(1,128)S(1)}, f32[1,256,10,1]{1,3,2,0:T(1,128)S(1)}, u32[]{:S(2)}, u32[]{:S(2)}) collective-permute-start(f32[1,256,10,1]{1,3,2,0:T(1,128)S(1)} %get-tuple-element.48), channel_id=1, source_target_pairs={{0,8},{8,16},{16,24},{24,32},{32,40},{40,48},{48,56},{56,64},{64,7... | collective-permute-start | bytes 30728 | tf_op jit(solution)/shard_map/ppermute | solution.py:15
  144.6 12.4 %collective-permute-start.7 = (f32[1,256,10,1]{1,3,2,0:T(1,128)S(1)}, f32[1,256,10,1]{1,3,2,0:T(1,128)S(1)}, u32[]{:S(2)}, u32[]{:S(2)}) collective-permute-start(f32[1,256,10,1]{1,3,2,0:T(1,128)S(1)} %get-tuple-element.49), channel_id=1, source_target_pairs={{8,0},{16,8},{24,16},{32,24},{40,32},{48,40},{56,48},{64,56},{72,6... | collective-permute-start | bytes 30728 | tf_op jit(solution)/shard_map/ppermute | solution.py:16
  150.4 9.3 %copy-start.21 = (f32[8]{0:T(128)}, f32[8]{0:T(128)S(1)}, u32[]{:S(2)}) copy-start(f32[8]{0:T(128)S(1)} %multiply_sine_fusion) | copy-start | bytes 100
  150.4 3.8 copy-start.10
  159.4 1.6 copy-start.7
  159.4 2.2 copy-start.14
  164.4 29.9 %copy-start.1 = (f32[1,256,8,256]{1,3,2,0:T(8,128)}, f32[1,256,8,256]{1,3,2,0:T(8,128)S(1)}, u32[]{:S(2)}) copy-start(f32[1,256,8,256]{1,3,2,0:T(8,128)S(1)} %get-tuple-element.27) | copy-start | bytes 6291460
  164.4 11.9 %copy-start.23 = (f32[1,1,256]{2,1,0:T(1,128)S(1)}, f32[1,1,256]{2,1,0:T(1,128)}, u32[]{:S(2)}) copy-start(f32[1,1,256]{2,1,0:T(1,128)} %param.11) | copy-start | bytes 3076
  164.5 29.8 %collective-permute-start.8 = (f32[2,256,1,256]{1,3,2,0:T(8,128)S(1)}, f32[2,256,1,256]{1,3,2,0:T(8,128)S(1)}, u32[]{:S(2)}, u32[]{:S(2)}) collective-permute-start(f32[2,256,1,256]{1,3,2,0:T(8,128)S(1)} %get-tuple-element.42), channel_id=1, source_target_pairs={{0,1},{1,2},{2,3},{3,4},{4,5},{5,6},{6,7},{8,9},{9,10},{10,11},{11... | collective-permute-start | bytes 1572872 | tf_op jit(solution)/shard_map/ppermute | solution.py:15
  170.8 23.5 %collective-permute-start.9 = (f32[2,256,1,256]{1,3,2,0:T(8,128)S(1)}, f32[2,256,1,256]{1,3,2,0:T(8,128)S(1)}, u32[]{:S(2)}, u32[]{:S(2)}) collective-permute-start(f32[2,256,1,256]{1,3,2,0:T(8,128)S(1)} %get-tuple-element.43), channel_id=1, source_target_pairs={{1,0},{2,1},{3,2},{4,3},{5,4},{6,5},{7,6},{9,8},{10,9},{11,10},{12... | collective-permute-start | bytes 1572872 | tf_op jit(solution)/shard_map/ppermute | solution.py:16
  194.4 21.6 %collective-permute-start.10 = (f32[2,256,10,1]{1,0,3,2:T(2,128)S(1)}, f32[2,256,10,1]{1,0,3,2:T(2,128)S(1)}, u32[]{:S(2)}, u32[]{:S(2)}) collective-permute-start(f32[2,256,10,1]{1,0,3,2:T(2,128)S(1)} %copy.49), channel_id=1, source_target_pairs={{0,8},{8,16},{16,24},{24,32},{32,40},{40,48},{48,56},{56,64},{64,7... | collective-permute-start | bytes 61448 | tf_op jit(solution)/shard_map/ppermute | solution.py:15
  194.5 21.5 %collective-permute-start.11 = (f32[2,256,10,1]{1,0,3,2:T(2,128)S(1)}, f32[2,256,10,1]{1,0,3,2:T(2,128)S(1)}, u32[]{:S(2)}, u32[]{:S(2)}) collective-permute-start(f32[2,256,10,1]{1,0,3,2:T(2,128)S(1)} %copy.50), channel_id=1, source_target_pairs={{8,0},{16,8},{24,16},{32,24},{40,32},{48,40},{56,48},{64,56},{72,6... | collective-permute-start | bytes 61448 | tf_op jit(solution)/shard_map/ppermute | solution.py:16
  218.2 1.6 copy-start.3
  220.5 14.9 %copy-start.16 = (pred[256]{0:T(512)(128)(4,1)S(1)}, pred[256]{0:T(512)(128)(4,1)}, u32[]{:S(2)}) copy-start(pred[256]{0:T(512)(128)(4,1)} %get-tuple-element.66) | copy-start | bytes 772
  220.5 15.1 %copy-start.20 = (f32[1,1,256]{2,1,0:T(1,128)S(1)}, f32[1,1,256]{2,1,0:T(1,128)}, u32[]{:S(2)}) copy-start(f32[1,1,256]{2,1,0:T(1,128)} %get-tuple-element.60) | copy-start | bytes 3076
  220.5 15.1 %copy-start.24 = (f32[1,1,256]{2,1,0:T(1,128)S(1)}, f32[1,1,256]{2,1,0:T(1,128)}, u32[]{:S(2)}) copy-start(f32[1,1,256]{2,1,0:T(1,128)} %param.10) | copy-start | bytes 3076
  220.5 15.1 %copy-start.17 = (f32[256]{0:T(256)S(1)}, f32[256]{0:T(256)}, u32[]{:S(2)}) copy-start(f32[256]{0:T(256)} %get-tuple-element.67) | copy-start | bytes 3076
  220.5 15.1 %copy-start.18 = (f32[1,1,256]{2,1,0:T(1,128)S(1)}, f32[1,1,256]{2,1,0:T(1,128)}, u32[]{:S(2)}) copy-start(f32[1,1,256]{2,1,0:T(1,128)} %get-tuple-element.61) | copy-start | bytes 3076
  221.3 24.3 %collective-permute-start.12 = (f32[1,256,1,256]{1,3,2,0:T(8,128)}, f32[1,256,1,256]{1,3,2,0:T(8,128)S(1)}, u32[]{:S(2)}, u32[]{:S(2)}) collective-permute-start(f32[1,256,1,256]{1,3,2,0:T(8,128)} %get-tuple-element.50), channel_id=1, source_target_pairs={{0,1},{1,2},{2,3},{3,4},{4,5},{5,6},{6,7},{8,9},{9,10},{10,11},{11... | collective-permute-start | bytes 786440 | tf_op jit(solution)/shard_map/ppermute | solution.py:15
  228.5 21.5 %collective-permute-start.13 = (f32[1,256,1,256]{1,3,2,0:T(8,128)}, f32[1,256,1,256]{1,3,2,0:T(8,128)S(1)}, u32[]{:S(2)}, u32[]{:S(2)}) collective-permute-start(f32[1,256,1,256]{1,3,2,0:T(8,128)} %get-tuple-element.51), channel_id=1, source_target_pairs={{1,0},{2,1},{3,2},{4,3},{5,4},{6,5},{7,6},{9,8},{10,9},{11,10},{12... | collective-permute-start | bytes 786440 | tf_op jit(solution)/shard_map/ppermute | solution.py:16
  237.2 384.6 %all-reduce.6.cloned.1.call-start = ((), (), s32[]{:S(2)}) async-start(), calls=%async_computation.1 | async-start | bytes 524288 | tf_op jit(solution)/shard_map/psum | solution.py:68
  250.4 1.5 copy-start.8
  251.9 262.1 %collective-permute-start.14 = (f32[1,256,10,1]{1,3,2,0:T(1,128)S(1)}, f32[1,256,10,1]{1,3,2,0:T(1,128)S(1)}, u32[]{:S(2)}, u32[]{:S(2)}) collective-permute-start(f32[1,256,10,1]{1,3,2,0:T(1,128)S(1)} %get-tuple-element.46), channel_id=1, source_target_pairs={{0,8},{8,16},{16,24},{24,32},{32,40},{40,48},{48,56},{56,64},{64,7... | collective-permute-start | bytes 30728 | tf_op jit(solution)/shard_map/ppermute | solution.py:15
  252.0 262.0 %collective-permute-start.15 = (f32[1,256,10,1]{1,3,2,0:T(1,128)S(1)}, f32[1,256,10,1]{1,3,2,0:T(1,128)S(1)}, u32[]{:S(2)}, u32[]{:S(2)}) collective-permute-start(f32[1,256,10,1]{1,3,2,0:T(1,128)S(1)} %get-tuple-element.47), channel_id=1, source_target_pairs={{8,0},{16,8},{24,16},{32,24},{40,32},{48,40},{56,48},{64,56},{72,6... | collective-permute-start | bytes 30728 | tf_op jit(solution)/shard_map/ppermute | solution.py:16
  518.8 1.6 copy-start.12
  518.8 2.2 copy-start.13
  518.8 2.2 copy-start.22
  522.2 1.4 copy-start.4
  522.2 2.0 copy-start.5
  524.2 136.3 %copy-start.25 = (s32[2]{0:T(128)S(1)}, s32[2]{0:T(128)}, u32[]{:S(2)}) copy-start(s32[2]{0:T(128)} %iota_multiply_fusion) | copy-start | bytes 28
Sparse Core Ops, SparseCore 0:
  237.3 276.5 all-reduce.3
  516.5 105.1 all-reduce.5
